TPU v7x, 32 devices: a whole 2x2x4 slice. The times are simulated.
32 devices in a mesh: nodes: 8 (over y, x, core), cols: 4 (over z).
Axes of the slice: x: 2, y: 2, z: 4, core: 2. Of those that a mesh axis runs over, the one named last changes fastest.
Arguments:
- features: bfloat16 [1024, 512], P('nodes', 'cols'), may hold values from -6 to 6
- weight: bfloat16 [512, 512], P(None, 'cols'), may hold values from -0.25 to 0.25
- degree: int32 [1024], P('nodes'), may hold values from 1 to 64
- tile_cols: int32 [8, 8], P('nodes'), may hold values from 0 to 7, as said below
- tile_count: int32 [8], P('nodes'), may hold values from 1 to 8, as said below
- tile_codes: int32 [8, 8], P('nodes'), may hold values from 0 to 1048575
- cotangent: bfloat16 [1024, 512], P('nodes', 'cols'), may hold values from -6 to 6
Outputs:
- activation: bfloat16 [1024, 512], P('nodes', 'cols')
- weight_grad: float32 [512, 512], P(None, 'cols')
- feats_grad: float32 [1024, 512], P('nodes', 'cols')
Inputs may be any that keep to these rules, and one draw needn't show every extreme that they name: `tile_cols`: each row lists every node block once, and row i begins with block i. The tiles of row block i are those of its first tile_count[i] slots; some row block holds all 8.
All inputs are finite; a program needn't handle non-finite values.
Results may differ from a plain program's by a relative error of at most 0.0065.
Values may be sent and summed in bfloat16 or wider, within the bound.
A program may use at most 64 MiB of HBM per device.

v0:
```python
import jax
import jax.numpy as jnp
from jax import lax
from jax.sharding import PartitionSpec as P

TILE = 128


def tile_bits(pattern_code):
    line_ids = jnp.arange(TILE, dtype=jnp.int32)
    hashed = (
        pattern_code[..., None, None] * 73856093
        ^ line_ids[:, None] * 19349663
        ^ line_ids[None, :] * 83492791
    )
    hashed = hashed ^ hashed >> 13
    hashed = hashed * 1274126177
    hashed = hashed ^ hashed >> 16
    return hashed & 63 == 0


def make_tiles(matches, code_table, live_limit, own, identity):
    slot_ids = jnp.arange(matches.shape[1], dtype=jnp.int32)
    slot_index = jnp.sum(jnp.where(matches, slot_ids[None, :], 0), axis=1, dtype=jnp.int32)
    code_value = jnp.sum(jnp.where(matches, code_table, 0), axis=1, dtype=jnp.int32)
    pattern = tile_bits(code_value) & (slot_index < live_limit)[:, None, None]
    values = (
        pattern.astype(jnp.float32)
        + jnp.where(own, 1.0, 0.0).astype(jnp.float32)[:, None, None] * identity
    )
    return values.astype(jnp.bfloat16)


def body(features, weight, degree, tile_cols, tile_count, tile_codes, cotangent):
    my_block = lax.axis_index("nodes")
    identity = jnp.eye(TILE, dtype=jnp.float32)
    inv_root = lax.rsqrt(degree.astype(jnp.float32))[:, None]
    scaled = (features.astype(jnp.float32) * inv_root).astype(jnp.bfloat16)
    my_cols = tile_cols[0]
    my_codes = tile_codes[0]
    my_count = tile_count[0]
    pieces = lax.all_gather(scaled[None], "nodes", axis=0, tiled=True)
    count_blocks = pieces.shape[0]
    targets = jnp.arange(count_blocks, dtype=jnp.int32)
    matches = targets[:, None] == my_cols[None, :]
    tiles = make_tiles(matches, my_codes[None, :], my_count, targets == my_block, identity)
    gathered = lax.dot_general(
        tiles, pieces, (((0, 2), (0, 1)), ((), ())), preferred_element_type=jnp.float32
    )
    aggregated = (inv_root * gathered).astype(jnp.bfloat16)
    agg_full = lax.all_gather(aggregated, "cols", axis=1, tiled=True)
    pre = jnp.dot(agg_full, weight, preferred_element_type=jnp.float32)
    activation = jax.nn.silu(pre).astype(jnp.bfloat16)
    sigma = jax.nn.sigmoid(pre)
    grad_pre = (cotangent.astype(jnp.float32) * sigma * (1.0 + pre * (1.0 - sigma))).astype(
        jnp.bfloat16
    )
    partial_grad = lax.dot_general(
        agg_full, grad_pre, (((0,), (0,)), ((), ())), preferred_element_type=jnp.float32
    )
    weight_grad = lax.psum(partial_grad, "nodes")
    terms = lax.dot_general(
        grad_pre, weight, (((1,), (1,)), ((), ())), preferred_element_type=jnp.float32
    )
    grad_agg = lax.psum_scatter(terms, "cols", scatter_dimension=1, tiled=True)
    grad_scaled = (inv_root * grad_agg).astype(jnp.bfloat16)
    all_cols, all_counts, all_codes = (
        lax.all_gather(tile_cols, "nodes", axis=0, tiled=True),
        lax.all_gather(tile_count, "nodes", axis=0, tiled=True),
        lax.all_gather(tile_codes, "nodes", axis=0, tiled=True),
    )
    pieces = lax.all_gather(grad_scaled[None], "nodes", axis=0, tiled=True)
    count_blocks = pieces.shape[0]
    row_ids = jnp.arange(count_blocks, dtype=jnp.int32)
    tiles = make_tiles(all_cols == my_block, all_codes, all_counts, row_ids == my_block, identity)
    back_total = lax.dot_general(
        tiles, pieces, (((0, 1), (0, 1)), ((), ())), preferred_element_type=jnp.float32
    )
    feats_grad = inv_root * back_total
    return (activation, weight_grad, feats_grad)


def solution(mesh):
    in_specs = (
        P("nodes", "cols"),
        P(None, "cols"),
        P("nodes"),
        P("nodes", None),
        P("nodes"),
        P("nodes", None),
        P("nodes", "cols"),
    )
    out_specs = (P("nodes", "cols"), P(None, "cols"), P("nodes", "cols"))
    return jax.shard_map(body, mesh=mesh, in_specs=in_specs, out_specs=out_specs, check_vma=False)
```

profile of v0, /device:TPU:0, one launch (start us, length us, event | category | flops | bytes accessed | tf_op | source)
XLA Modules:
  0.0 118.2 jit_solution(6654077568115102820)
XLA Ops:
  8.0 0.0 copy-start
  8.0 0.0 reduce-scatter.2.cloned.1.call-start
  8.1 0.0 copy-start.2
  8.1 0.0 copy-start.4
  8.1 0.6 copy-done.4
  8.8 10.2 %all-gather.2 = s32[8,1,8]{2,1,0:T(1,128)S(1)} all-gather(s32[1,1,8]{2,1,0:T(1,128)S(1)} %bitcast.36), channel_id=1, replica_groups=mesh['nodes'=8,'cols'=4] {'nodes'}, dimensions={0}, use_global_device_ids=true | all-gather | bytes 288 | tf_op jit(solution)/shard_map/all_gather | solution.py:68
  19.0 0.7 copy-done.3
  19.6 8.8 %all-gather.3 = s32[8,1,8]{2,1,0:T(1,128)S(1)} all-gather(s32[1,1,8]{2,1,0:T(1,128)S(1)} %bitcast.34), channel_id=1, replica_groups=mesh['nodes'=8,'cols'=4] {'nodes'}, dimensions={0}, use_global_device_ids=true | all-gather | bytes 288 | tf_op jit(solution)/shard_map/all_gather | solution.py:70
  28.5 0.1 multiply_convert_fusion.3
  28.6 8.3 %all-gather = bf16[1024,128]{1,0:T(8,128)(2,1)S(1)} all-gather(bf16[128,128]{1,0:T(8,128)(2,1)S(1)} %multiply_convert_fusion.3), channel_id=2, replica_groups=mesh['nodes'=8,'cols'=4] {'nodes'}, dimensions={0}, use_global_device_ids=true | all-gather | bytes 294912 | tf_op jit(solution)/shard_map/all_gather | solution.py:42
  37.6 0.1 select_reduce_fusion
  37.7 0.2 select_reduce_fusion.2
  37.9 0.1 broadcast_xor_fusion
  38.0 0.5 fusion.2
  38.5 12.5 %all_gather.19 = bf16[128,512]{1,0:T(8,128)(2,1)S(1)} all-gather(bf16[128,128]{1,0:T(8,128)(2,1)S(1)} %fusion.2), channel_id=1, replica_groups=mesh['nodes'=8,'cols'=4] {'cols'}, dimensions={1}, use_global_device_ids=true | all-gather | bytes 163840 | tf_op jit(solution)/shard_map/all_gather | solution.py:51
  51.0 0.8 multiply_convert_fusion.2
  51.8 0.9 fusion.46
  52.7 0.0 reduce-scatter.2.cloned.1.call-update
  52.7 0.0 all-reduce.3.cloned.1.call-start
  52.7 0.0 copy-start.6
  52.8 0.6 copy-done.6
  53.4 0.6 dynamic-slice
  54.0 0.8 dynamic-update-slice
  54.7 0.9 fusion.47
  55.7 0.0 all-reduce.3.cloned.1.call-update
  55.7 7.4 %all-reduce = s32[8]{0:T(128)S(1)} all-reduce(s32[8]{0:T(128)S(1)} %dynamic-update-slice), channel_id=1, replica_groups=mesh['nodes'=8,'cols'=4] {'nodes'}, use_global_device_ids=true, to_apply=%add | all-reduce | flops 8 | bytes 64
  63.1 8.6 %reduce-scatter.2.cloned.1.call-done = f32[128,128]{1,0:T(8,128)} async-done(((f32[128,512]{1,0:T(8,128)}), f32[128,128]{1,0:T(8,128)}) %reduce-scatter.2.cloned.1.call-update) | async-done | bytes 65552 | tf_op jit(solution)/shard_map/reduce_scatter | solution.py:65
  71.7 0.9 multiply_convert_fusion
  72.6 9.5 %all-gather.1 = bf16[1024,128]{1,0:T(8,128)(2,1)S(1)} all-gather(bf16[128,128]{1,0:T(8,128)(2,1)S(1)} %multiply_convert_fusion), channel_id=3, replica_groups=mesh['nodes'=8,'cols'=4] {'nodes'}, dimensions={0}, use_global_device_ids=true | all-gather | bytes 294912 | tf_op jit(solution)/shard_map/all_gather | solution.py:72
  82.1 1.1 fusion
  83.1 26.0 %all-reduce.3.cloned.1.call-done = f32[512,128]{1,0:T(8,128)} async-done(((f32[512,128]{1,0:T(8,128)}), f32[512,128]{1,0:T(8,128)}) %all-reduce.3.cloned.1.call-update) | async-done | bytes 262160 | tf_op jit(solution)/shard_map/psum | solution.py:61
  109.1 1.7 %copy.18 = f32[512,128]{1,0:T(8,128)} copy(f32[512,128]{1,0:T(8,128)} %all-reduce.3.cloned.1.call-done) | data formatting | bytes 524288
  (16 shorter events, 0.1 us)
Async XLA Ops:
  8.0 43.0 %copy-start = (bf16[512,128]{1,0:T(8,128)(2,1)S(1)}, bf16[512,128]{1,0:T(8,128)(2,1)}, u32[]{:S(2)}) copy-start(bf16[512,128]{1,0:T(8,128)(2,1)} %param.8) | copy-start | bytes 393220
  8.0 63.7 %reduce-scatter.2.cloned.1.call-start = ((), (), s32[]{:S(2)}) async-start(), calls=%async_computation.2 | async-start | bytes 327680 | tf_op jit(solution)/shard_map/reduce_scatter | solution.py:65
  8.1 20.4 %copy-start.2 = (bf16[128,128]{1,0:T(8,128)(2,1)S(1)}, bf16[128,128]{1,0:T(8,128)(2,1)}, u32[]{:S(2)}) copy-start(bf16[128,128]{1,0:T(8,128)(2,1)} %param.7) | copy-start | bytes 98308
  8.1 0.7 copy-start.4
  19.0 0.7 copy-start.3
  19.6 8.8 %copy-start.5 = (s32[128]{0:T(128)S(1)}, s32[128]{0:T(128)}, u32[]{:S(2)}) copy-start(s32[128]{0:T(128)} %param.9) | copy-start | bytes 1540
  51.0 0.8 copy-start.1
  52.7 56.4 %all-reduce.3.cloned.1.call-start = ((), (), s32[]{:S(2)}) async-start(), calls=%async_computation.1 | async-start | bytes 524288 | tf_op jit(solution)/shard_map/psum | solution.py:61
  52.7 0.7 copy-start.6
Sparse Core Ops, SparseCore 0:
  52.8 18.8 reduce-scatter.1
Sparse Core Ops, SparseCore 1:
  56.8 52.3 all-reduce.2
where the time goes:
time: 119 us; the launch traced here: 118 us
  blocking collectives  56.7 us (48%)
  waiting for transfers between devices  34.7 us (29%)
  between operations  16.2 us (14%)
  local copies, waits for them, and re-layouts  4.98 us (4%)
  matrix products  4.16 us (3%)
  other arithmetic  1.41 us (1%)
    psum x1, waiting for transfers between devices, body(): weight_grad = lax.psum(partial_grad, 'nodes')  26 us
    all_gather x1, blocking collectives, body(): agg_full = lax.all_gather(aggregated, 'cols', axis=1, tiled=True)  12.5 us
    all_gather x1, blocking collectives, body(): lax.all_gather(tile_cols, 'nodes', axis=0, tiled=True)  10.2 us
    all_gather x1, blocking collectives, body(): pieces = lax.all_gather(grad_scaled[None], 'nodes', axis=0, tiled=True)  9.48 us
    all_gather x1, blocking collectives, body(): lax.all_gather(tile_codes, 'nodes', axis=0, tiled=True)  8.84 us
    reduce_scatter x1, waiting for transfers between devices, body(): grad_agg = lax.psum_scatter(terms, 'cols', scatter_dimension=1, tiled=True)  8.63 us
    all_gather x1, blocking collectives, body(): pieces = lax.all_gather(scaled[None], 'nodes', axis=0, tiled=True)  8.34 us
    unnamed x1, blocking collectives  7.36 us
  transfers between devices with their start and end apart: 2, of which 2 were waited for; matrix products, arithmetic and copies ran while one was open for 4% of the time, Pallas kernels for 0%

commit v1 on v0

--- a/solution.py
+++ b/solution.py
@@ -1,7 +1,13 @@
+import functools
+
 import jax
 import jax.numpy as jnp
 from jax import lax
+from jax.experimental import pallas as pl
+from jax.experimental.pallas import tpu as pltpu
 from jax.sharding import PartitionSpec as P
+
+MESH = pl.DeviceIdType.MESH
 
 TILE = 128
 
@@ -80,6 +86,183 @@
     return (activation, weight_grad, feats_grad)
 
 
+FUSED_NODES = 8
+
+
+def dot(a, b, dims):
+    return lax.dot_general(a, b, (dims, ((), ())), preferred_element_type=jnp.float32)
+
+
+def hash_tile(code, base, own, identity):
+    shape = base.shape
+    hashed = (code * 73856093)[None] ^ base.reshape(shape[0] // 8, 8, shape[1])
+    hashed = hashed ^ hashed >> 13
+    hashed = hashed * 1274126177
+    hashed = hashed ^ hashed >> 16
+    bits = jnp.where((hashed & 63 == 0) & (code >= 0)[None], 1.0, 0.0).reshape(shape)
+    return (bits + jnp.where(own, 1.0, 0.0) * identity).astype(jnp.bfloat16)
+
+
+def fused_kernel(
+    nodes, cols,
+    features, weight, degree, tile_cols, tile_count, tile_codes, cotangent,
+    activation, weight_grad, feats_grad,
+    feat_all, agg_all, gp_all, gs_all, w_all, tab_out, tab_in, fwd_tiles, bwd_tiles,
+    wg_part, wg_in, wg_all,
+    feat_send, feat_recv, tab_send, tab_recv, w_send, w_recv, agg_send, agg_recv,
+    gp_send, gp_recv, gs_send, gs_recv, rs_send, rs_recv, ag_send, ag_recv,
+):
+    n = lax.axis_index("nodes")
+    c = lax.axis_index("cols")
+    node_peers = [(lax.rem(n + d, nodes), c) for d in range(1, nodes)]
+    col_peers = [(n, lax.rem(c + d, cols)) for d in range(1, cols)]
+
+    barrier = pltpu.get_barrier_semaphore()
+    for peer in node_peers + col_peers:
+        pl.semaphore_signal(barrier, inc=1, device_id=peer, device_id_type=MESH)
+
+    def push(src, dst, peer, send, recv):
+        copy = pltpu.make_async_remote_copy(
+            src_ref=src, dst_ref=dst, send_sem=send, recv_sem=recv, device_id=peer, device_id_type=MESH
+        )
+        copy.start()
+        return copy
+
+    def gather(buffer, me, peers, send, recv):
+        return [
+            push(buffer.at[me], buffer.at[me], peer, send.at[i], recv.at[i]) for i, peer in enumerate(peers)
+        ]
+
+    row_ids = lax.broadcasted_iota(jnp.int32, (TILE, TILE), 0)
+    lane_ids = lax.broadcasted_iota(jnp.int32, (TILE, TILE), 1)
+    identity = jnp.where(row_ids == lane_ids, 1.0, 0.0)
+    inv_row = lax.rsqrt(degree[...].astype(jnp.float32))
+    inv_root = jnp.sum(identity * inv_row, axis=1, keepdims=True)
+    feat_all[n] = (features[...].astype(jnp.float32) * inv_root).astype(jnp.bfloat16)
+
+    codes = []
+    for block in range(nodes):
+        code = jnp.int32(-1)
+        for slot in range(nodes):
+            hit = (tile_cols[0, slot] == block) & (slot < tile_count[0])
+            code = jnp.where(hit, tile_codes[0, slot], code)
+        codes.append(jnp.full((8, TILE), code, jnp.int32))
+        tab_out[block] = codes[-1]
+
+    pl.semaphore_wait(barrier, nodes + cols - 2)
+
+    feat_copies = gather(feat_all, n, node_peers, feat_send, feat_recv)
+    tab_copies = [
+        push(tab_out.at[peer[0]], tab_in.at[n], peer, tab_send.at[i], tab_recv.at[i])
+        for i, peer in enumerate(node_peers)
+    ]
+    w_copies = [
+        push(
+            weight.at[pl.ds(pl.multiple_of(peer[1] * TILE, TILE), TILE), :],
+            w_all.at[c], peer, w_send.at[i], w_recv.at[i],
+        )
+        for i, peer in enumerate(col_peers)
+    ]
+    w_all[c] = weight[pl.ds(pl.multiple_of(c * TILE, TILE), TILE), :]
+    tab_in[n] = tab_out[n]
+
+    base = row_ids * 19349663 ^ lane_ids * 83492791
+    for block in range(nodes):
+        fwd_tiles[:, block * TILE:(block + 1) * TILE] = hash_tile(codes[block], base, n == block, identity)
+
+    for copy in feat_copies:
+        copy.wait_recv()
+    gathered = dot(fwd_tiles[...], feat_all[...].reshape(nodes * TILE, TILE), ((1,), (0,)))
+    agg_all[c] = (inv_root * gathered).astype(jnp.bfloat16)
+    agg_copies = gather(agg_all, c, col_peers, agg_send, agg_recv)
+
+    for copy in tab_copies:
+        copy.wait_recv()
+    base_t = lane_ids * 19349663 ^ row_ids * 83492791
+    for block in range(nodes):
+        bwd_tiles[:, block * TILE:(block + 1) * TILE] = hash_tile(tab_in[block], base_t, n == block, identity)
+
+    for copy in agg_copies:
+        copy.wait_recv()
+    pre = dot(agg_all[0], weight[:TILE, :], ((1,), (0,)))
+    for q in range(1, cols):
+        pre += dot(agg_all[q], weight[q * TILE:(q + 1) * TILE, :], ((1,), (0,)))
+    sigma = jax.nn.sigmoid(pre)
+    grad_pre = (cotangent[...].astype(jnp.float32) * sigma * (1.0 + pre * (1.0 - sigma))).astype(jnp.bfloat16)
+    gp_all[c] = grad_pre
+    gp_copies = gather(gp_all, c, col_peers, gp_send, gp_recv)
+
+    rows = wg_part.shape[1]
+    for q in range(cols):
+        part = dot(agg_all[q], grad_pre, ((0,), (0,)))
+        for i in range(TILE // rows):
+            wg_part[q * (TILE // rows) + i] = part[i * rows:(i + 1) * rows, :]
+    rs_copies = [
+        push(wg_part.at[peer[0]], wg_in.at[n], peer, rs_send.at[i], rs_recv.at[i])
+        for i, peer in enumerate(node_peers)
+    ]
+    wg_in[n] = wg_part[n]
+    activation[...] = (pre * sigma).astype(jnp.bfloat16)
+
+    for copy in w_copies + gp_copies:
+        copy.wait_recv()
+    grad_agg = dot(gp_all[0], w_all[0], ((1,), (1,)))
+    for q in range(1, cols):
+        grad_agg += dot(gp_all[q], w_all[q], ((1,), (1,)))
+    gs_all[n] = (inv_root * grad_agg).astype(jnp.bfloat16)
+    gs_copies = gather(gs_all, n, node_peers, gs_send, gs_recv)
+
+    for copy in rs_copies:
+        copy.wait_recv()
+    wg_all[n] = jnp.sum(wg_in[...], axis=0).astype(wg_all.dtype)
+    ag_copies = gather(wg_all, n, node_peers, ag_send, ag_recv)
+
+    for copy in gs_copies:
+        copy.wait_recv()
+    back = dot(bwd_tiles[...], gs_all[...].reshape(nodes * TILE, TILE), ((1,), (0,)))
+    feats_grad[...] = inv_root * back
+
+    for copy in ag_copies:
+        copy.wait_recv()
+    for block in range(nodes):
+        weight_grad[block * rows:(block + 1) * rows, :] = wg_all[block].astype(jnp.float32)
+    for copy in feat_copies + tab_copies + w_copies + agg_copies + gp_copies + rs_copies + gs_copies + ag_copies:
+        copy.wait_send()
+
+
+def fused(nodes, cols, features, weight, degree, tile_cols, tile_count, tile_codes, cotangent):
+    rows = weight.shape[0] // nodes
+    vmem = pl.BlockSpec(memory_space=pltpu.VMEM)
+    smem = pl.BlockSpec(memory_space=pltpu.SMEM)
+    block = (TILE, TILE)
+    sems = [pltpu.SemaphoreType.DMA((count - 1,)) for count in (nodes, nodes, cols, cols, cols, nodes, nodes, nodes) for _ in "sr"]
+    return pl.pallas_call(
+        functools.partial(fused_kernel, nodes, cols),
+        out_shape=(
+            jax.ShapeDtypeStruct(features.shape, jnp.bfloat16),
+            jax.ShapeDtypeStruct(weight.shape, jnp.float32),
+            jax.ShapeDtypeStruct(features.shape, jnp.float32),
+        ),
+        in_specs=[vmem, vmem, vmem, smem, smem, smem, vmem],
+        out_specs=(vmem, vmem, vmem),
+        scratch_shapes=[
+            pltpu.VMEM((nodes,) + block, jnp.bfloat16),
+            pltpu.VMEM((cols,) + block, jnp.bfloat16),
+            pltpu.VMEM((cols,) + block, jnp.bfloat16),
+            pltpu.VMEM((nodes,) + block, jnp.bfloat16),
+            pltpu.VMEM((cols,) + block, jnp.bfloat16),
+            pltpu.VMEM((nodes, 8, TILE), jnp.int32),
+            pltpu.VMEM((nodes, 8, TILE), jnp.int32),
+            pltpu.VMEM((TILE, nodes * TILE), jnp.bfloat16),
+            pltpu.VMEM((TILE, nodes * TILE), jnp.bfloat16),
+            pltpu.VMEM((nodes, rows, TILE), jnp.float32),
+            pltpu.VMEM((nodes, rows, TILE), jnp.float32),
+            pltpu.VMEM((nodes, rows, TILE), jnp.bfloat16),
+        ] + sems,
+        compiler_params=pltpu.CompilerParams(collective_id=0, has_side_effects=True),
+    )(features, weight, degree[None, :], tile_cols, tile_count, tile_codes, cotangent)
+
+
 def solution(mesh):
     in_specs = (
         P("nodes", "cols"),
@@ -91,4 +274,7 @@
         P("nodes", "cols"),
     )
     out_specs = (P("nodes", "cols"), P(None, "cols"), P("nodes", "cols"))
-    return jax.shard_map(body, mesh=mesh, in_specs=in_specs, out_specs=out_specs, check_vma=False)
+    local = body
+    if mesh.shape["nodes"] <= FUSED_NODES:
+        local = functools.partial(fused, mesh.shape["nodes"], mesh.shape["cols"])
+    return jax.shard_map(local, mesh=mesh, in_specs=in_specs, out_specs=out_specs, check_vma=False)

time: 119 us -> 32.7 us (0.27)
  blocking collectives: 56.7 us -> 0 us
  waiting for transfers between devices: 34.7 us -> 0 us
  Pallas kernels: 0 us -> 27.5 us
  between operations: 16.2 us -> 1.29 us
  matrix products: 4.16 us -> 0 us
  other arithmetic: 1.41 us -> 0 us
  local copies, waits for them, and re-layouts: 4.98 us -> 3.71 us
    all_gather x5 -> x0, blocking collectives: 49.3 us -> none  [the longest x1 12.5 us: body(): agg_full = lax.all_gather(aggregated, 'cols', axis=1, tiled=True)]
    pallas_call x0 -> x1, Pallas kernels: none -> 27.5 us  [fused(): pl.pallas_call(functools.partial(fused_kernel, nodes, cols), out_shape=(j...]
    psum x1 -> x0, waiting for transfers between devices: 26 us -> none  [body(): weight_grad = lax.psum(partial_grad, 'nodes')]
    reduce_scatter x1 -> x0, waiting for transfers between devices: 8.63 us -> none  [body(): grad_agg = lax.psum_scatter(terms, 'cols', scatter_dimension=1, tiled=True)]
    unnamed x1 -> x0, blocking collectives: 7.36 us -> none
    dot_general x5 -> x0, matrix products: 4.16 us -> none  [the longest x1 1.05 us: body(): lax.dot_general(tiles, pieces, (((0, 1), (0, 1)), ((), ())), preferred_el...]
    unnamed x18 -> x5, local copies, waits for them, and re-layouts: 4.98 us -> 3.71 us
  transfers between devices with their start and end apart: 2 -> 0, of which waited for: 2 -> 0; matrix products, arithmetic and copies ran while one was open for 4% -> 0% of each run, Pallas kernels for 0% -> 0%
where the time goes in v1:
time: 32.7 us; the launch traced here: 32.5 us
  Pallas kernels  27.5 us (84%)
  local copies, waits for them, and re-layouts  3.71 us (11%)
  between operations  1.29 us (4%)
    pallas_call x1, Pallas kernels, fused(): pl.pallas_call(functools.partial(fused_kernel, nodes, cols), out_shape=(j...  27.5 us
    unnamed x5, local copies, waits for them, and re-layouts  3.71 us

profile of v1, /device:TPU:0, one launch (start us, length us, event | category | flops | bytes accessed | tf_op | source)
XLA Modules:
  0.0 32.5 jit_solution(2229429177637011596)
XLA Ops:
  1.3 27.5 %shard_map.94 = (bf16[128,128]{1,0:T(8,128)(2,1)}, f32[512,128]{1,0:T(8,128)}, f32[128,128]{1,0:T(8,128)}) custom-call(bf16[128,128]{1,0:T(8,128)(2,1)} %features.1, bf16[512,128]{1,0:T(8,128)(2,1)} %weight.1, s32[1,128]{1,0:T(1,128)} %bitcast.1, s32[1,8]{1,0:T(1,128)} %tile_cols.1, s32[1]{0:T(128)S(6)} %copy.13.tile_count, s32[1,8]{1,0:T(1,128)} %tile_codes.1, ...), custom_call_target="tpu_custom_call" | custom-call | tf_op jit(solution)/shard_map/pallas_call | solution.py:239
  28.8 1.4 %copy.14 = bf16[128,128]{1,0:T(8,128)(2,1)} copy(bf16[128,128]{1,0:T(8,128)(2,1)} %get-tuple-element.6) | data formatting | bytes 65536
  30.1 0.0 copy-start
  30.1 1.7 %copy.15 = f32[512,128]{1,0:T(8,128)} copy(f32[512,128]{1,0:T(8,128)} %get-tuple-element.7) | data formatting | bytes 524288
  31.8 0.0 copy-done
  31.8 0.6 %copy.16 = f32[128,128]{1,0:T(8,128)} copy(f32[128,128]{1,0:T(8,128)S(1)} %copy-done) | data formatting | bytes 131072
Async XLA Ops:
  30.1 1.7 %copy-start = (f32[128,128]{1,0:T(8,128)S(1)}, f32[128,128]{1,0:T(8,128)}, u32[]{:S(2)}) copy-start(f32[128,128]{1,0:T(8,128)} %get-tuple-element.8) | copy-start | bytes 196612

commit v2 on v1

--- a/solution.py
+++ b/solution.py
@@ -94,64 +94,94 @@
 
 
 def hash_tile(code, base, own, identity):
-    shape = base.shape
-    hashed = (code * 73856093)[None] ^ base.reshape(shape[0] // 8, 8, shape[1])
+    hashed = (code * 73856093) ^ base
     hashed = hashed ^ hashed >> 13
     hashed = hashed * 1274126177
     hashed = hashed ^ hashed >> 16
-    bits = jnp.where((hashed & 63 == 0) & (code >= 0)[None], 1.0, 0.0).reshape(shape)
+    bits = jnp.where((hashed & 63 == 0) & (code >= 0), 1.0, 0.0)
     return (bits + jnp.where(own, 1.0, 0.0) * identity).astype(jnp.bfloat16)
 
 
 def fused_kernel(
     nodes, cols,
+    features_hbm, weight_hbm, degree_hbm, tile_cols_hbm, tile_count_hbm, tile_codes_hbm, cotangent_hbm,
+    activation, weight_grad, feats_grad,
     features, weight, degree, tile_cols, tile_count, tile_codes, cotangent,
-    activation, weight_grad, feats_grad,
     feat_all, agg_all, gp_all, gs_all, w_all, tab_out, tab_in, fwd_tiles, bwd_tiles,
-    wg_part, wg_in, wg_all,
-    feat_send, feat_recv, tab_send, tab_recv, w_send, w_recv, agg_send, agg_recv,
-    gp_send, gp_recv, gs_send, gs_recv, rs_send, rs_recv, ag_send, ag_recv,
+    wg_part, wg_pair, wg_half, wg_in, wg_all,
+    load_sem, feat_send, feat_recv, tab_send, tab_recv, w_send, w_recv, agg_send, agg_recv,
+    gp_send, gp_recv, gs_send, gs_recv, pair_send, pair_recv, rs_send, rs_recv, ag_send, ag_recv,
 ):
     n = lax.axis_index("nodes")
     c = lax.axis_index("cols")
+    chips = nodes // 2
+    chip, core = n // 2, lax.rem(n, 2)
+    partner = n + 1 - 2 * core
     node_peers = [(lax.rem(n + d, nodes), c) for d in range(1, nodes)]
     col_peers = [(n, lax.rem(c + d, cols)) for d in range(1, cols)]
+    twins = [lax.rem(n + 2 * d, nodes) for d in range(1, chips)]
+    senders = [lax.rem(n + nodes - 2 * d, nodes) for d in range(1, chips)]
 
     barrier = pltpu.get_barrier_semaphore()
     for peer in node_peers + col_peers:
         pl.semaphore_signal(barrier, inc=1, device_id=peer, device_id_type=MESH)
+
+    loads = []
+    for i, (src, dst) in enumerate((
+        (degree_hbm, degree), (features_hbm, features), (tile_cols_hbm, tile_cols), (tile_count_hbm, tile_count),
+        (tile_codes_hbm, tile_codes), (weight_hbm, weight), (cotangent_hbm, cotangent),
+    )):
+        loads.append(pltpu.make_async_copy(src, dst, load_sem.at[i]))
+        loads[-1].start()
+
+    sent = []
 
     def push(src, dst, peer, send, recv):
         copy = pltpu.make_async_remote_copy(
             src_ref=src, dst_ref=dst, send_sem=send, recv_sem=recv, device_id=peer, device_id_type=MESH
         )
         copy.start()
+        sent.append(copy)
         return copy
 
-    def gather(buffer, me, peers, send, recv):
-        return [
-            push(buffer.at[me], buffer.at[me], peer, send.at[i], recv.at[i]) for i, peer in enumerate(peers)
-        ]
+    def push_block(buffer, slot, peer, i, send, recv):
+        return push(buffer.at[slot], buffer.at[slot], peer, send.at[i], recv.at[i])
+
+    def spread(buffer, send, recv):
+        far = [push_block(buffer, n, (twin, c), i, send, recv) for i, twin in enumerate(twins)]
+        return far, [push_block(buffer, n, (partner, c), chips - 1, send, recv)]
+
+    def pass_on(buffer, far, near, send, recv):
+        for i, sender in enumerate(senders):
+            far[i].wait_recv()
+            near.append(push_block(buffer, sender, (partner, c), chips + i, send, recv))
+
+    def gather_cols(buffer, send, recv):
+        return [push_block(buffer, c, peer, i, send, recv) for i, peer in enumerate(col_peers)]
 
     row_ids = lax.broadcasted_iota(jnp.int32, (TILE, TILE), 0)
     lane_ids = lax.broadcasted_iota(jnp.int32, (TILE, TILE), 1)
     identity = jnp.where(row_ids == lane_ids, 1.0, 0.0)
+    base = row_ids * 19349663 ^ lane_ids * 83492791
+    loads[0].wait()
     inv_row = lax.rsqrt(degree[...].astype(jnp.float32))
     inv_root = jnp.sum(identity * inv_row, axis=1, keepdims=True)
+    loads[1].wait()
     feat_all[n] = (features[...].astype(jnp.float32) * inv_root).astype(jnp.bfloat16)
 
-    codes = []
+    for load in loads[2:5]:
+        load.wait()
     for block in range(nodes):
         code = jnp.int32(-1)
         for slot in range(nodes):
             hit = (tile_cols[0, slot] == block) & (slot < tile_count[0])
             code = jnp.where(hit, tile_codes[0, slot], code)
-        codes.append(jnp.full((8, TILE), code, jnp.int32))
-        tab_out[block] = codes[-1]
+        tab_out[block] = jnp.full((1, TILE), code, jnp.int32)
+    loads[5].wait()
 
     pl.semaphore_wait(barrier, nodes + cols - 2)
 
-    feat_copies = gather(feat_all, n, node_peers, feat_send, feat_recv)
+    feat_far, feat_near = spread(feat_all, feat_send, feat_recv)
     tab_copies = [
         push(tab_out.at[peer[0]], tab_in.at[n], peer, tab_send.at[i], tab_recv.at[i])
         for i, peer in enumerate(node_peers)
@@ -166,21 +196,22 @@
     w_all[c] = weight[pl.ds(pl.multiple_of(c * TILE, TILE), TILE), :]
     tab_in[n] = tab_out[n]
 
-    base = row_ids * 19349663 ^ lane_ids * 83492791
     for block in range(nodes):
-        fwd_tiles[:, block * TILE:(block + 1) * TILE] = hash_tile(codes[block], base, n == block, identity)
-
-    for copy in feat_copies:
+        fwd_tiles[:, block * TILE:(block + 1) * TILE] = hash_tile(tab_out[block], base, n == block, identity)
+
+    pass_on(feat_all, feat_far, feat_near, feat_send, feat_recv)
+    for copy in feat_near:
         copy.wait_recv()
     gathered = dot(fwd_tiles[...], feat_all[...].reshape(nodes * TILE, TILE), ((1,), (0,)))
     agg_all[c] = (inv_root * gathered).astype(jnp.bfloat16)
-    agg_copies = gather(agg_all, c, col_peers, agg_send, agg_recv)
+    agg_copies = gather_cols(agg_all, agg_send, agg_recv)
 
     for copy in tab_copies:
         copy.wait_recv()
     base_t = lane_ids * 19349663 ^ row_ids * 83492791
     for block in range(nodes):
         bwd_tiles[:, block * TILE:(block + 1) * TILE] = hash_tile(tab_in[block], base_t, n == block, identity)
+    loads[6].wait()
 
     for copy in agg_copies:
         copy.wait_recv()
@@ -190,19 +221,22 @@
     sigma = jax.nn.sigmoid(pre)
     grad_pre = (cotangent[...].astype(jnp.float32) * sigma * (1.0 + pre * (1.0 - sigma))).astype(jnp.bfloat16)
     gp_all[c] = grad_pre
-    gp_copies = gather(gp_all, c, col_peers, gp_send, gp_recv)
-
-    rows = wg_part.shape[1]
+    gp_copies = gather_cols(gp_all, gp_send, gp_recv)
+
+    rows = wg_in.shape[1]
     for q in range(cols):
         part = dot(agg_all[q], grad_pre, ((0,), (0,)))
         for i in range(TILE // rows):
-            wg_part[q * (TILE // rows) + i] = part[i * rows:(i + 1) * rows, :]
+            owner = q * (TILE // rows) + i
+            wg_part[owner % 2, owner // 2] = part[i * rows:(i + 1) * rows, :]
+    pair = push(wg_part.at[1 - core], wg_pair, (partner, c), pair_send, pair_recv)
+    activation[...] = (pre * sigma).astype(jnp.bfloat16)
+    pair.wait_recv()
+    wg_half[...] = wg_part[core] + wg_pair[...]
     rs_copies = [
-        push(wg_part.at[peer[0]], wg_in.at[n], peer, rs_send.at[i], rs_recv.at[i])
-        for i, peer in enumerate(node_peers)
+        push(wg_half.at[twin // 2], wg_in.at[i], (twin, c), rs_send.at[i], rs_recv.at[i])
+        for i, twin in enumerate(twins)
     ]
-    wg_in[n] = wg_part[n]
-    activation[...] = (pre * sigma).astype(jnp.bfloat16)
 
     for copy in w_copies + gp_copies:
         copy.wait_recv()
@@ -210,57 +244,95 @@
     for q in range(1, cols):
         grad_agg += dot(gp_all[q], w_all[q], ((1,), (1,)))
     gs_all[n] = (inv_root * grad_agg).astype(jnp.bfloat16)
-    gs_copies = gather(gs_all, n, node_peers, gs_send, gs_recv)
+    gs_far, gs_near = spread(gs_all, gs_send, gs_recv)
 
     for copy in rs_copies:
         copy.wait_recv()
-    wg_all[n] = jnp.sum(wg_in[...], axis=0).astype(wg_all.dtype)
-    ag_copies = gather(wg_all, n, node_peers, ag_send, ag_recv)
-
-    for copy in gs_copies:
+    wg_all[n] = (wg_half[chip] + jnp.sum(wg_in[...], axis=0)).astype(wg_all.dtype)
+    ag_far, ag_near = spread(wg_all, ag_send, ag_recv)
+
+    pass_on(gs_all, gs_far, gs_near, gs_send, gs_recv)
+    pass_on(wg_all, ag_far, ag_near, ag_send, ag_recv)
+    for copy in gs_near:
         copy.wait_recv()
     back = dot(bwd_tiles[...], gs_all[...].reshape(nodes * TILE, TILE), ((1,), (0,)))
     feats_grad[...] = inv_root * back
 
-    for copy in ag_copies:
+    for copy in ag_near:
         copy.wait_recv()
     for block in range(nodes):
         weight_grad[block * rows:(block + 1) * rows, :] = wg_all[block].astype(jnp.float32)
-    for copy in feat_copies + tab_copies + w_copies + agg_copies + gp_copies + rs_copies + gs_copies + ag_copies:
+    for copy in sent:
         copy.wait_send()
+
+
+def write_out_kernel(*refs):
+    count = len(refs) // 2
+    copies = [pltpu.make_async_copy(refs[i], refs[count + i], refs[-1].at[i]) for i in range(count)]
+    for copy in copies:
+        copy.start()
+    for copy in copies:
+        copy.wait()
 
 
 def fused(nodes, cols, features, weight, degree, tile_cols, tile_count, tile_codes, cotangent):
     rows = weight.shape[0] // nodes
+    chips = nodes // 2
+    anywhere = pl.BlockSpec(memory_space=pl.ANY)
     vmem = pl.BlockSpec(memory_space=pltpu.VMEM)
-    smem = pl.BlockSpec(memory_space=pltpu.SMEM)
     block = (TILE, TILE)
-    sems = [pltpu.SemaphoreType.DMA((count - 1,)) for count in (nodes, nodes, cols, cols, cols, nodes, nodes, nodes) for _ in "sr"]
-    return pl.pallas_call(
+    outs = ((features.shape, jnp.bfloat16), (weight.shape, jnp.float32), (features.shape, jnp.float32))
+    hops = 2 * chips - 1
+    dma = pltpu.SemaphoreType.DMA
+    results = pl.pallas_call(
         functools.partial(fused_kernel, nodes, cols),
-        out_shape=(
-            jax.ShapeDtypeStruct(features.shape, jnp.bfloat16),
-            jax.ShapeDtypeStruct(weight.shape, jnp.float32),
-            jax.ShapeDtypeStruct(features.shape, jnp.float32),
-        ),
-        in_specs=[vmem, vmem, vmem, smem, smem, smem, vmem],
+        out_shape=tuple(pltpu.VMEM(shape, dtype) for shape, dtype in outs),
+        in_specs=[anywhere] * 7,
         out_specs=(vmem, vmem, vmem),
         scratch_shapes=[
+            pltpu.VMEM(features.shape, jnp.bfloat16),
+            pltpu.VMEM(weight.shape, jnp.bfloat16),
+            pltpu.VMEM((1, TILE), jnp.int32),
+            pltpu.SMEM(tile_cols.shape, jnp.int32),
+            pltpu.SMEM(tile_count.shape, jnp.int32),
+            pltpu.SMEM(tile_codes.shape, jnp.int32),
+            pltpu.VMEM(cotangent.shape, jnp.bfloat16),
             pltpu.VMEM((nodes,) + block, jnp.bfloat16),
             pltpu.VMEM((cols,) + block, jnp.bfloat16),
             pltpu.VMEM((cols,) + block, jnp.bfloat16),
             pltpu.VMEM((nodes,) + block, jnp.bfloat16),
             pltpu.VMEM((cols,) + block, jnp.bfloat16),
-            pltpu.VMEM((nodes, 8, TILE), jnp.int32),
-            pltpu.VMEM((nodes, 8, TILE), jnp.int32),
+            pltpu.VMEM((nodes, 1, TILE), jnp.int32),
+            pltpu.VMEM((nodes, 1, TILE), jnp.int32),
             pltpu.VMEM((TILE, nodes * TILE), jnp.bfloat16),
             pltpu.VMEM((TILE, nodes * TILE), jnp.bfloat16),
-            pltpu.VMEM((nodes, rows, TILE), jnp.float32),
-            pltpu.VMEM((nodes, rows, TILE), jnp.float32),
+            pltpu.VMEM((2, chips, rows, TILE), jnp.float32),
+            pltpu.VMEM((chips, rows, TILE), jnp.float32),
+            pltpu.VMEM((chips, rows, TILE), jnp.float32),
+            pltpu.VMEM((chips - 1, rows, TILE), jnp.float32),
             pltpu.VMEM((nodes, rows, TILE), jnp.bfloat16),
-        ] + sems,
+            dma((7,)),
+            dma((hops,)), dma((hops,)),
+            dma((nodes - 1,)), dma((nodes - 1,)),
+            dma((cols - 1,)), dma((cols - 1,)),
+            dma((cols - 1,)), dma((cols - 1,)),
+            dma((cols - 1,)), dma((cols - 1,)),
+            dma((hops,)), dma((hops,)),
+            dma, dma,
+            dma((chips - 1,)), dma((chips - 1,)),
+            dma((hops,)), dma((hops,)),
+        ],
         compiler_params=pltpu.CompilerParams(collective_id=0, has_side_effects=True),
+        name="layer",
     )(features, weight, degree[None, :], tile_cols, tile_count, tile_codes, cotangent)
+    return pl.pallas_call(
+        write_out_kernel,
+        out_shape=tuple(jax.ShapeDtypeStruct(shape, dtype) for shape, dtype in outs),
+        in_specs=[vmem] * 3,
+        out_specs=(anywhere,) * 3,
+        scratch_shapes=[dma((3,))],
+        name="write_out",
+    )(*[pltpu.with_memory_space_constraint(x, pltpu.VMEM) for x in results])
 
 
 def solution(mesh):

time: 32.7 us -> 27.3 us (0.83)
  local copies, waits for them, and re-layouts: 3.71 us -> 0 us
  Pallas kernels: 27.5 us -> 25.9 us
    unnamed x5 -> x0, local copies, waits for them, and re-layouts: 3.71 us -> none
    pallas_call x1 -> x2, Pallas kernels: 27.5 us -> 25.9 us  [the longest x1 25.1 us: fused(): pl.pallas_call(functools.partial(fused_kernel, nodes, cols), out_shape=tu...]
where the time goes in v2:
time: 27.3 us; the launch traced here: 27.1 us
  Pallas kernels  25.9 us (95%)
  between operations  1.29 us (5%)
    pallas_call x1, Pallas kernels, fused(): pl.pallas_call(functools.partial(fused_kernel, nodes, cols), out_shape=tu...  25.1 us
    pallas_call x1, Pallas kernels, fused(): pl.pallas_call(write_out_kernel, out_shape=tuple((jax.ShapeDtypeStruct(sh...  0.76 us

profile of v2, /device:TPU:0, one launch (start us, length us, event | category | flops | bytes accessed | tf_op | source)
XLA Modules:
  0.0 27.1 jit_solution(10116072150172577689)
XLA Ops:
  1.3 25.1 %layer.1 = (bf16[128,128]{1,0:T(8,128)(2,1)S(1)}, f32[512,128]{1,0:T(8,128)S(1)}, f32[128,128]{1,0:T(8,128)S(1)}) custom-call(bf16[128,128]{1,0:T(8,128)(2,1)} %features_hbm.1, bf16[512,128]{1,0:T(8,128)(2,1)} %weight_hbm.1, s32[1,128]{1,0:T(1,128)} %bitcast.1, s32[1,8]{1,0:T(1,128)} %tile_cols_hbm.1, s32[1]{0:T(128)S(6)} %copy.10.tile_count_hbm, ...), custom_call_target="tpu_custom_call" | custom-call | tf_op jit(solution)/shard_map/layer/pallas_call | solution.py:287
  26.4 0.8 %write_out.1 = (bf16[128,128]{1,0:T(8,128)(2,1)}, f32[512,128]{1,0:T(8,128)}, f32[128,128]{1,0:T(8,128)}) custom-call(bf16[128,128]{1,0:T(8,128)(2,1)S(1)} %get-tuple-element.6.refs_0_, f32[512,128]{1,0:T(8,128)S(1)} %get-tuple-element.7.refs_1_, f32[128,128]{1,0:T(8,128)S(1)} %get-tuple-element.8.refs_2_), custom_call_target="tpu_custom_call" | custom-call | tf_op jit(solution)/shard_map/write_out/pallas_call | solution.py:328

commit v3 on v2

--- a/solution.py
+++ b/solution.py
@@ -249,10 +249,9 @@
     for copy in rs_copies:
         copy.wait_recv()
     wg_all[n] = (wg_half[chip] + jnp.sum(wg_in[...], axis=0)).astype(wg_all.dtype)
-    ag_far, ag_near = spread(wg_all, ag_send, ag_recv)
+    ag_near = [push_block(wg_all, n, peer, i, ag_send, ag_recv) for i, peer in enumerate(node_peers)]
 
     pass_on(gs_all, gs_far, gs_near, gs_send, gs_recv)
-    pass_on(wg_all, ag_far, ag_near, ag_send, ag_recv)
     for copy in gs_near:
         copy.wait_recv()
     back = dot(bwd_tiles[...], gs_all[...].reshape(nodes * TILE, TILE), ((1,), (0,)))

time: 27.3 us -> 27.2 us (level)
  Pallas kernels: 25.9 us -> 25.5 us
    pallas_call x1, Pallas kernels: 25.1 us -> 24.8 us  [fused(): pl.pallas_call(functools.partial(fused_kernel, nodes, cols), out_shape=tu...]
where the time goes in v3:
time: 27.2 us; the launch traced here: 26.8 us
  Pallas kernels  25.5 us (94%)
  between operations  1.29 us (5%)
    pallas_call x1, Pallas kernels, fused(): pl.pallas_call(functools.partial(fused_kernel, nodes, cols), out_shape=tu...  24.8 us
    pallas_call x1, Pallas kernels, fused(): pl.pallas_call(write_out_kernel, out_shape=tuple((jax.ShapeDtypeStruct(sh...  0.76 us

profile of v3, /device:TPU:0, one launch (start us, length us, event | category | flops | bytes accessed | tf_op | source)
XLA Modules:
  0.0 26.8 jit_solution(8257898359783695327)
XLA Ops:
  1.3 24.8 %layer.1 = (bf16[128,128]{1,0:T(8,128)(2,1)S(1)}, f32[512,128]{1,0:T(8,128)S(1)}, f32[128,128]{1,0:T(8,128)S(1)}) custom-call(bf16[128,128]{1,0:T(8,128)(2,1)} %features_hbm.1, bf16[512,128]{1,0:T(8,128)(2,1)} %weight_hbm.1, s32[1,128]{1,0:T(1,128)} %bitcast.1, s32[1,8]{1,0:T(1,128)} %tile_cols_hbm.1, s32[1]{0:T(128)S(6)} %copy.10.tile_count_hbm, ...), custom_call_target="tpu_custom_call" | custom-call | tf_op jit(solution)/shard_map/layer/pallas_call | solution.py:286
  26.1 0.8 %write_out.1 = (bf16[128,128]{1,0:T(8,128)(2,1)}, f32[512,128]{1,0:T(8,128)}, f32[128,128]{1,0:T(8,128)}) custom-call(bf16[128,128]{1,0:T(8,128)(2,1)S(1)} %get-tuple-element.6.refs_0_, f32[512,128]{1,0:T(8,128)S(1)} %get-tuple-element.7.refs_1_, f32[128,128]{1,0:T(8,128)S(1)} %get-tuple-element.8.refs_2_), custom_call_target="tpu_custom_call" | custom-call | tf_op jit(solution)/shard_map/write_out/pallas_call | solution.py:327
